TPU v7x, 32 devices: a whole 2x2x4 slice. The times are simulated.
32 devices in a mesh: row: 4 (over y, x), col: 8 (over z, core).
Axes of the slice: x: 2, y: 2, z: 4, core: 2. Of those that a mesh axis runs over, the one named last changes fastest.
Arguments:
- pointmaps: bfloat16 [64, 64, 2, 3, 14336], P('row', 'col'), may hold values from -6 to 6
- confidence: bfloat16 [64, 64, 2, 14336], P('row', 'col'), may hold values from 1 to 10
- valid_blocks: int32 [64, 64, 64], P('row', 'col'), may hold values 0 or 1
- log_depth: float32 [64, 14336], P('row', 'col'), may hold values from 0 to 1.4
- camera: float32 [64, 8], replicated, may hold values from -1 to 5.8, as said below
- pair_pose: float32 [64, 64, 8], P('row', 'col'), may hold values from -1 to 1.2, as said below
- step_sizes: float32 [3], replicated, may hold values from 0.02 to 0.2
Outputs:
- new_log_depth: float32 [64, 14336], P('row', 'col')
- new_camera: float32 [64, 8], replicated
- new_pair_pose: float32 [64, 64, 8], P('row', 'col')
Inputs may be any that keep to these rules, and one draw needn't show every extreme that they name: `camera`: columns 0 to 3 hold a quaternion whose first entry lies in 0.8 to 1.2 and the others in -0.3 to 0.3; columns 4 to 6 a translation in -1 to 1; column 7 a log focal length in pixels, 5.2 to 5.8. `pair_pose`: columns 0 to 3 hold a quaternion whose first entry lies in 0.8 to 1.2 and the others in -0.3 to 0.3; columns 4 to 6 a translation in -1 to 1; column 7 a log scale in -0.5 to 0.5.
All inputs are finite; a program needn't handle non-finite values. No bound on the sum of `valid_blocks` on one device may be relied on, other than what follows from the above.
Results may differ from a plain program's by a relative error of at most 0.00055.
Values sent between devices are 32-bit elements; how exact they have to be, the bound alone decides.
No kernel may reach another device: no remote copies, remote signals or barrier semaphores. Data moves between devices by JAX's collectives and lax.ppermute only.
A program may use at most 192 MiB of HBM per device.

v0:
```python
import functools

import numpy as np

import jax
import jax.numpy as jnp
from jax import lax
from jax.experimental import pallas as pl
from jax.experimental.pallas import tpu as pltpu
from jax.sharding import PartitionSpec as P

IMAGES = 64
IMG_WIDTH = 224
IMG_HEIGHT = 224
WIN_ROWS = 64
ADAM_STEPS = 2

BETA_ONE = 0.9
BETA_TWO = 0.999
ADAM_EPS = 0.001
SOFTEN = 0.01

LANES = 128
SUBLANES = 8
TABLE_PAIRS = 64


def rotation(quaternion):
    length = jnp.sqrt(jnp.sum(quaternion * quaternion, axis=-1))
    w = quaternion[..., 0] / length
    x = quaternion[..., 1] / length
    y = quaternion[..., 2] / length
    z = quaternion[..., 3] / length
    return [
        [1.0 - 2.0 * (y * y + z * z), 2.0 * (x * y - w * z), 2.0 * (x * z + w * y)],
        [2.0 * (x * y + w * z), 1.0 - 2.0 * (x * x + z * z), 2.0 * (y * z - w * x)],
        [2.0 * (x * z - w * y), 2.0 * (y * z + w * x), 1.0 - 2.0 * (x * x + y * y)],
    ]


def adam_step(param, grad, first, second, step_number, step_size):
    first = BETA_ONE * first + (1.0 - BETA_ONE) * grad
    second = BETA_TWO * second + (1.0 - BETA_TWO) * grad * grad
    update = (
        step_size
        * (first / (1.0 - BETA_ONE**step_number))
        / (jnp.sqrt(second / (1.0 - BETA_TWO**step_number)) + ADAM_EPS)
    )
    return (param - update, first, second)


def world_points(log_depths, cameras):
    pixel_count = log_depths.shape[-1]
    position = jnp.arange(pixel_count, dtype=jnp.int32)
    across = (position % IMG_WIDTH).astype(jnp.float32) - (IMG_WIDTH - 1) / 2.0
    downward = (position // IMG_WIDTH + (IMG_HEIGHT - WIN_ROWS) // 2).astype(jnp.float32) - (
        IMG_HEIGHT - 1
    ) / 2.0
    focal_len = jnp.exp(cameras[:, 7:8])
    depth_map = jnp.exp(log_depths)
    ray_parts = (
        across[None, :] / focal_len * depth_map,
        downward[None, :] / focal_len * depth_map,
        depth_map,
    )
    turned = rotation(cameras[:, 0:4])
    return [
        turned[k][0][:, None] * ray_parts[0]
        + turned[k][1][:, None] * ray_parts[1]
        + turned[k][2][:, None] * ray_parts[2]
        + cameras[:, 4 + k][:, None]
        for k in range(3)
    ]


def pair_loss(
    first_depth,
    second_depth,
    first_camera,
    second_camera,
    pair_params,
    pointmaps,
    confidence,
    valid_blocks,
    first_ids,
    second_ids,
):
    first_world = world_points(first_depth, first_camera)
    second_world = world_points(second_depth, second_camera)
    pair_rotation = rotation(pair_params[..., 0:4])
    pair_scale = jnp.exp(pair_params[..., 7])
    pair_keep = (first_ids[:, None] != second_ids[None, :]).astype(jnp.float32)
    pixel_keep = (
        jnp.repeat(valid_blocks.astype(jnp.float32), IMG_WIDTH, axis=2) * pair_keep[:, :, None]
    )
    loss_sum = jnp.zeros((), jnp.float32)
    for side_index in range(2):
        if side_index == 0:
            points_side = [first_world[k][:, None, :] for k in range(3)]
        else:
            points_side = [second_world[k][None, :, :] for k in range(3)]
        source = [pointmaps[:, :, side_index, k, :].astype(jnp.float32) for k in range(3)]
        squared = SOFTEN
        for k in range(3):
            aligned = (
                pair_scale[..., None]
                * (
                    pair_rotation[k][0][..., None] * source[0]
                    + pair_rotation[k][1][..., None] * source[1]
                    + pair_rotation[k][2][..., None] * source[2]
                )
                + pair_params[..., 4 + k][..., None]
            )
            residual = points_side[k] - aligned
            squared = squared + residual * residual
        weight = confidence[:, :, side_index, :].astype(jnp.float32) * pixel_keep
        loss_sum = loss_sum + jnp.sum(weight * jnp.sqrt(squared))
    return loss_sum / (2.0 * (IMAGES - 1))


def general_body(pointmaps, confidence, valid_blocks, log_depth, camera, pair_pose, step_sizes):
    row_count = pointmaps.shape[0]
    col_count = pointmaps.shape[1]
    row_index = lax.axis_index("row")
    col_index = lax.axis_index("col")
    first_ids = row_index * row_count + jnp.arange(row_count, dtype=jnp.int32)
    second_ids = col_index * col_count + jnp.arange(col_count, dtype=jnp.int32)

    def local_loss(row_depth, col_depth, cameras, pair_params):
        first_camera = lax.dynamic_slice_in_dim(cameras, row_index * row_count, row_count, 0)
        second_camera = lax.dynamic_slice_in_dim(cameras, col_index * col_count, col_count, 0)
        return pair_loss(
            row_depth,
            col_depth,
            first_camera,
            second_camera,
            pair_params,
            pointmaps,
            confidence,
            valid_blocks,
            first_ids,
            second_ids,
        )

    depth_now, camera_now, pair_now = (log_depth, camera, pair_pose)
    depth_first = jnp.zeros_like(log_depth)
    depth_second = jnp.zeros_like(log_depth)
    camera_first = jnp.zeros_like(camera)
    camera_second = jnp.zeros_like(camera)
    pair_first = jnp.zeros_like(pair_pose)
    pair_second = jnp.zeros_like(pair_pose)
    for step_number in range(1, ADAM_STEPS + 1):
        row_depth = lax.all_gather(depth_now, "col", axis=1, tiled=True)
        every_image = lax.all_gather(depth_now, "row", axis=0, tiled=True)
        col_depth = lax.all_to_all(every_image, "col", split_axis=0, concat_axis=1, tiled=True)
        row_grad, col_grad, cam_grad, pair_grad = jax.grad(local_loss, argnums=(0, 1, 2, 3))(
            row_depth, col_depth, camera_now, pair_now
        )
        returned = lax.all_to_all(col_grad, "col", split_axis=1, concat_axis=0, tiled=True)
        from_cols = lax.psum_scatter(returned, "row", scatter_dimension=0, tiled=True)
        depth_grad = lax.psum_scatter(row_grad, "col", scatter_dimension=1, tiled=True)
        depth_grad = depth_grad + from_cols
        cam_total = lax.psum(cam_grad, ("row", "col"))
        depth_now, depth_first, depth_second = adam_step(
            depth_now, depth_grad, depth_first, depth_second, step_number, step_sizes[0]
        )
        camera_now, camera_first, camera_second = adam_step(
            camera_now, cam_total, camera_first, camera_second, step_number, step_sizes[1]
        )
        pair_now, pair_first, pair_second = adam_step(
            pair_now, pair_grad, pair_first, pair_second, step_number, step_sizes[2]
        )
    return (depth_now, camera_now, pair_now)


def pick_lanes(values, index):
    numbers = lax.GatherDimensionNumbers(
        offset_dims=(),
        collapsed_slice_dims=(1,),
        start_index_map=(1,),
        operand_batching_dims=(0,),
        start_indices_batching_dims=(0,),
    )
    return lax.gather(
        values,
        index[..., None],
        numbers,
        slice_sizes=(1, 1),
        mode=lax.GatherScatterMode.PROMISE_IN_BOUNDS,
    )


def cross(a, b):
    return [
        a[1] * b[2] - a[2] * b[1],
        a[2] * b[0] - a[0] * b[2],
        a[0] * b[1] - a[1] * b[0],
    ]


def grad_kernel(shape, step, *refs):
    rows, cols, slots, row_slots, tile = shape
    n_dep = slots + row_slots
    refs = list(refs)
    me, pair, cam, rate, x_ref, conf_ref, table, lane_base, ray = refs[:9]
    depth_refs = refs[9 : 9 + n_dep]
    at = 9 + n_dep
    grad_refs = None
    if step > 1:
        grad_refs = refs[at : at + n_dep]
        at += n_dep
    keep_out, send_out = refs[at : at + 2]
    col_out = refs[at + 2 : at + 2 + row_slots]
    at += 2 + row_slots
    pair_out, cam_out = refs[at : at + 2]
    chi_i, chi_j, grad_i, grad_j, wide = refs[at + 2 :]

    i = pl.program_id(0)
    my_row, my_col = me[0], me[1]
    core = my_col & 1
    n_tiles = chi_i.shape[1]

    def depth_of(slot, start):
        take = pl.ds(start, tile, stride=SUBLANES)
        value = depth_refs[slot][take, :]
        if step > 1:
            g = grad_refs[slot][take, :]
            value = value - rate[0] * g / (jnp.abs(g) + ADAM_EPS)
        return jnp.exp(value)

    def put_points(dst, image, slot, start, block):
        depth = depth_of(slot, start)
        across = ray[0, block] / cam[12, image] * depth
        downward = ray[1, block] / cam[12, image] * depth
        for k in range(3):
            value = (
                cam[3 * k, image] * across
                + cam[3 * k + 1, image] * downward
                + cam[3 * k + 2, image] * depth
                + cam[9 + k, image]
            )
            dst[k, pl.ds(block * tile, tile), :] = value

    def finish(points, grads, image, block, sums):
        take = pl.ds(block * tile, tile)
        g = [grads[k, take, :] for k in range(3)]
        v = [points[k, take, :] - cam[9 + k, image] for k in range(3)]
        axis = [cam[3 * k + 2, image] for k in range(3)]
        by_depth = g[0] * v[0] + g[1] * v[1] + g[2] * v[2]
        depth = axis[0] * v[0] + axis[1] * v[1] + axis[2] * v[2]
        along = axis[0] * g[0] + axis[1] * g[1] + axis[2] * g[2]
        new = g + cross(v, g) + [by_depth - depth * along]
        return by_depth, [s + n for s, n in zip(sums, new)]

    def stack_sums(sums):
        parts = [jnp.sum(s, axis=0, keepdims=True) for s in sums]
        return jnp.concatenate(parts + [jnp.zeros((1, LANES), jnp.float32)], axis=0)

    def add_camera(image, sums):
        total = jnp.sum(stack_sums(sums), axis=1, keepdims=True)
        lane = lax.broadcasted_iota(jnp.int32, (SUBLANES, LANES), 1)
        cam_out[...] += jnp.where(lane == image, total, 0.0)

    def col_block(e, k_slot):
        return (my_row ^ e) * 2 + (k_slot ^ core)

    @pl.when(i == 0)
    def _():
        def one(j, carry):
            for e in range(row_slots):
                for k_slot in range(2):
                    put_points(
                        chi_j.at[j],
                        my_col * cols + j,
                        slots + e,
                        k_slot * tile * SUBLANES + j,
                        col_block(e, k_slot),
                    )
            return carry

        lax.fori_loop(0, cols, one, 0)
        grad_j[...] = jnp.zeros_like(grad_j)
        cam_out[...] = jnp.zeros_like(cam_out)

    t, m = i // SUBLANES, i % SUBLANES
    for d in range(slots):
        block = my_col ^ d
        t_slot = t ^ core ^ (d & 1)
        put_points(
            chi_i, my_row * rows + i, d, t_slot * tile * SUBLANES + m, block
        )
    grad_i[...] = jnp.zeros_like(grad_i)

    both = 2 * SUBLANES

    def one_pair(j, carry):
        q = i * cols + j
        shift = [pair[j, 9 + k, i] for k in range(3)]
        scale = pair[j, 12, i]
        which = q // TABLE_PAIRS
        lane_at = q % TABLE_PAIRS
        turn = [pair[j, n, i] for n in range(9)]

        def one_chunk(ch, sums):
            packed = pl.ds(pl.multiple_of(ch * both, both), both)
            take = pl.ds(pl.multiple_of(ch * SUBLANES, SUBLANES), SUBLANES)
            for k in range(3):
                wide[k, packed, :] = x_ref[0, j, k, packed, :].astype(jnp.float32)
            wide[3, packed, :] = conf_ref[0, j, packed, :].astype(jnp.float32)
            keep = pick_lanes(table[which, take, :], lane_base[take, :] + lane_at)
            for side, points, grads in ((0, chi_i, grad_i), (1, chi_j.at[j], grad_j.at[j])):
                alternate = pl.ds(ch * both + side, SUBLANES, stride=2)
                x = [wide[k, alternate, :] for k in range(3)]
                weight = wide[3, alternate, :] * keep
                y, r = [], []
                squared = SOFTEN
                for k in range(3):
                    y.append(
                        turn[3 * k] * x[0] + turn[3 * k + 1] * x[1] + turn[3 * k + 2] * x[2]
                    )
                    r.append(points[k, take, :] - (scale * y[k] + shift[k]))
                    squared = squared + r[k] * r[k]
                scaled = weight * lax.rsqrt(squared)
                g = [scaled * r[k] for k in range(3)]
                for k in range(3):
                    grads[k, take, :] += g[k]
                trace = g[0] * y[0] + g[1] * y[1] + g[2] * y[2]
                new = g + cross(g, y) + [trace]
                sums = tuple(s + n for s, n in zip(sums, new))
            return sums

        zero = jnp.zeros((SUBLANES, LANES), jnp.float32)
        sums = lax.fori_loop(0, n_tiles // SUBLANES, one_chunk, (zero,) * 7, unroll=True)
        pair_out[0, j] = stack_sums(sums)
        return carry

    lax.fori_loop(0, cols, one_pair, 0)

    zero = jnp.zeros((tile, LANES), jnp.float32)
    sums = [zero] * 7
    for d in range(slots):
        block = my_col ^ d
        t_slot = t ^ core ^ (d & 1)
        value, sums = finish(chi_i, grad_i, my_row * rows + i, block, sums)
        out = send_out if d & 1 else keep_out
        start = (d // 2) * (2 * tile * SUBLANES) + t_slot * tile * SUBLANES + m
        out[pl.ds(start, tile, stride=SUBLANES), :] = value
    add_camera(my_row * rows + i, sums)

    @pl.when(i == rows - 1)
    def _():
        def one(j, carry):
            sums = [zero] * 7
            for e in range(row_slots):
                for k_slot in range(2):
                    value, sums = finish(
                        chi_j.at[j], grad_j.at[j], my_col * cols + j, col_block(e, k_slot), sums
                    )
                    start = k_slot * tile * SUBLANES + j
                    col_out[e][pl.ds(start, tile, stride=SUBLANES), :] = value
            add_camera(my_col * cols + j, sums)
            return carry

        lax.fori_loop(0, cols, one, 0)


def grads_of_pairs(step, sizes, me, pair, cam, rate, x, conf, table, consts, depths, totals):
    rows, cols, slots, row_slots, tile = sizes
    n_rows = 2 * slots * tile
    smem = pl.BlockSpec(memory_space=pltpu.SMEM)
    vmem = pl.BlockSpec(memory_space=pltpu.VMEM)
    operands = [me, pair, cam, rate, x, conf, table, *consts, *depths]
    if step > 1:
        operands += totals
    in_specs = [smem] * 4 + [
        pl.BlockSpec((1, cols, 3, n_rows, LANES), lambda i: (i, 0, 0, 0, 0)),
        pl.BlockSpec((1, cols, n_rows, LANES), lambda i: (i, 0, 0, 0)),
    ]
    in_specs += [vmem] * (len(operands) - len(in_specs))
    block = 2 * tile * SUBLANES
    f32 = jnp.float32
    out_shape = [
        jax.ShapeDtypeStruct((slots // 2 * block, LANES), f32),
        jax.ShapeDtypeStruct((slots // 2 * block, LANES), f32),
        *[jax.ShapeDtypeStruct((block, LANES), f32)] * row_slots,
        jax.ShapeDtypeStruct((rows, cols, SUBLANES, LANES), f32),
        jax.ShapeDtypeStruct((SUBLANES, LANES), f32),
    ]
    out_specs = [vmem] * (2 + row_slots) + [
        pl.BlockSpec((1, cols, SUBLANES, LANES), lambda i: (i, 0, 0, 0)),
        vmem,
    ]
    work = rows * cols * 3 * n_rows * LANES
    return pl.pallas_call(
        functools.partial(grad_kernel, sizes, step),
        grid=(rows,),
        in_specs=in_specs,
        out_specs=out_specs,
        out_shape=out_shape,
        scratch_shapes=[
            pltpu.VMEM((3, n_rows // 2, LANES), f32),
            pltpu.VMEM((cols, 3, n_rows // 2, LANES), f32),
            pltpu.VMEM((3, n_rows // 2, LANES), f32),
            pltpu.VMEM((cols, 3, n_rows // 2, LANES), f32),
            pltpu.VMEM((4, n_rows, LANES), f32),
        ],
        compiler_params=pltpu.CompilerParams(
            dimension_semantics=("arbitrary",), vmem_limit_bytes=52 * 1024 * 1024
        ),
        cost_estimate=pl.CostEstimate(
            flops=20 * work, bytes_accessed=3 * work, transcendentals=work // 3
        ),
    )(*operands)


def rotation_of(q):
    length = jnp.sqrt(q[0] * q[0] + q[1] * q[1] + q[2] * q[2] + q[3] * q[3])
    w, x, y, z = (part / length for part in q)
    return [
        1.0 - 2.0 * (y * y + z * z),
        2.0 * (x * y - w * z),
        2.0 * (x * z + w * y),
        2.0 * (x * y + w * z),
        1.0 - 2.0 * (x * x + z * z),
        2.0 * (y * z - w * x),
        2.0 * (x * z - w * y),
        2.0 * (y * z + w * x),
        1.0 - 2.0 * (x * x + y * y),
    ]


def quaternion_grad(q, torque):
    w, v = q[0], q[1:4]
    factor = 2.0 / (w * w + v[0] * v[0] + v[1] * v[1] + v[2] * v[2])
    c = cross(torque, v)
    real = -(torque[0] * v[0] + torque[1] * v[1] + torque[2] * v[2])
    return [factor * real] + [factor * (w * torque[k] + c[k]) for k in range(3)]


def pair_grads(p, s):
    scale = jnp.exp(p[7])
    parts = quaternion_grad(p, [scale * s[k] for k in (3, 4, 5)])
    return parts + [-s[0], -s[1], -s[2], -scale * s[6]]


def camera_grads(p, s):
    return quaternion_grad(p, s[3:6]) + [s[0], s[1], s[2], -s[6]]


def update_kernel(grads_of, step, n_sums, axes, *refs):
    refs = list(refs)
    rate, params = refs[:2]

    def at(ref, k):
        return ref.at[:, k, :] if axes == 3 else ref.at[pl.ds(k, 1), :]

    p = [at(params, k)[...] for k in range(8)]
    rest = refs[2:]
    if step:
        width = p[0].shape[-1]
        parts = []
        for sums in rest[:n_sums]:
            top = sums.shape[-2] - SUBLANES
            if axes == 3:
                parts.append([sums[:, k, :] for k in range(7)])
            else:
                parts.append([sums[pl.ds(top + k, 1), pl.ds(0, width)] for k in range(7)])
        total = [tree_sum([part[k] for part in parts]) for k in range(7)]
        g = grads_of(p, total)
        rest = rest[n_sums:]
        first, second = [jnp.zeros_like(v) for v in p], [jnp.zeros_like(v) for v in p]
        if step > 1:
            first = [at(rest[0], k)[...] for k in range(8)]
            second = [at(rest[1], k)[...] for k in range(8)]
            rest = rest[2:]
        for k in range(8):
            p[k], first[k], second[k] = adam_step(p[k], g[k], first[k], second[k], step, rate[0])
            at(rest[0], k)[...] = p[k]
            if step < ADAM_STEPS:
                at(rest[1], k)[...] = first[k]
                at(rest[2], k)[...] = second[k]
        rest = rest[3:] if step < ADAM_STEPS else rest[1:]
    if step < ADAM_STEPS:
        values = rotation_of(p[0:4]) + p[4:7] + [jnp.exp(p[7])]
        for k, value in enumerate(values):
            at(rest[0], k)[...] = value


def update(grads_of, step, rate, params, sums, state):
    f32 = jnp.float32
    like = jax.ShapeDtypeStruct(params.shape, f32)
    coef_shape = (*params.shape[:-2], 16, params.shape[-1])
    out_shape = []
    if step:
        out_shape += [like] * (3 if step < ADAM_STEPS else 1)
    if step < ADAM_STEPS:
        out_shape.append(jax.ShapeDtypeStruct(coef_shape, f32))
    vmem = pl.BlockSpec(memory_space=pltpu.VMEM)
    operands = [params, *sums, *(state if step > 1 else [])]
    outs = pl.pallas_call(
        functools.partial(update_kernel, grads_of, step, len(sums), params.ndim),
        in_specs=[pl.BlockSpec(memory_space=pltpu.SMEM)] + [vmem] * len(operands),
        out_specs=[vmem] * len(out_shape),
        out_shape=out_shape,
        compiler_params=pltpu.CompilerParams(vmem_limit_bytes=4 * 1024 * 1024),
        cost_estimate=pl.CostEstimate(flops=10000, bytes_accessed=100000, transcendentals=0),
    )
    outs = outs(rate, *operands)
    if not step:
        return params, [], outs[0]
    if step < ADAM_STEPS:
        return outs[0], outs[1:3], outs[3]
    return outs[0], [], None


def pixel_constants(n_tiles, blocks):
    pixel = np.arange(n_tiles * LANES).reshape(n_tiles, LANES)
    line = pixel // IMG_WIDTH
    across = (pixel % IMG_WIDTH).astype(np.float32) - np.float32((IMG_WIDTH - 1) / 2.0)
    downward = (line + (IMG_HEIGHT - WIN_ROWS) // 2).astype(np.float32) - np.float32(
        (IMG_HEIGHT - 1) / 2.0
    )
    ray = np.stack([across, downward]).reshape(2, blocks, n_tiles // blocks, LANES)
    first = line[:, 0]
    base = (line != first[:, None]).astype(np.int32) * TABLE_PAIRS
    lines = np.stack([first, np.minimum(first + 1, WIN_ROWS - 1)])
    pick = (lines[:, :, None] == np.arange(WIN_ROWS)).astype(np.float32)
    return jnp.asarray(base), jnp.asarray(ray), pick


def tree_sum(parts):
    while len(parts) > 1:
        parts = [a + b for a, b in zip(parts[::2], parts[1::2])]
    return parts[0]


def xor_permute(value, axis, bit, size):
    return lax.ppermute(value, axis, [(c, c ^ bit) for c in range(size)])


def fast_body(n_row, n_col, pointmaps, confidence, valid_blocks, log_depth, camera, pair_pose, step_sizes):
    rows, cols = pointmaps.shape[:2]
    pixels = pointmaps.shape[4]
    n_tiles = pixels // LANES
    tile = n_tiles // n_col
    sizes = (rows, cols, n_col, n_row, tile)
    row_index = lax.axis_index("row")
    col_index = lax.axis_index("col")
    core = col_index % 2
    me = jnp.stack([row_index, col_index]).astype(jnp.int32)
    f32 = jnp.float32

    x = pointmaps.transpose(0, 1, 3, 2, 4).reshape(rows, cols, 3, 2, n_tiles, LANES)
    x = x.transpose(0, 1, 2, 4, 3, 5).reshape(rows, cols, 3, 2 * n_tiles, LANES)
    conf = confidence.reshape(rows, cols, 2, n_tiles, LANES)
    conf = conf.transpose(0, 1, 3, 2, 4).reshape(rows, cols, 2 * n_tiles, LANES)

    base, ray, pick = pixel_constants(n_tiles, n_col)
    first_ids = row_index * rows + jnp.arange(rows, dtype=jnp.int32)
    second_ids = col_index * cols + jnp.arange(cols, dtype=jnp.int32)
    different = (first_ids[:, None] != second_ids[None, :]).astype(f32)
    share = different / (2.0 * (IMAGES - 1))
    valid = (valid_blocks.astype(f32)).reshape(rows * cols, WIN_ROWS)
    picked = lax.dot_general(
        jnp.asarray(pick.reshape(-1, WIN_ROWS)), valid, (((1,), (1,)), ((), ()))
    )
    picked = picked * share.reshape(1, rows * cols)
    picked = picked.reshape(2, n_tiles, rows * cols // TABLE_PAIRS, TABLE_PAIRS)
    table = picked.transpose(2, 1, 0, 3).reshape(-1, n_tiles, 2 * TABLE_PAIRS)

    def relative(value):
        return jnp.where(core == 0, value, value[::-1])

    def swap_perm(m):
        pairs = []
        for r in range(n_row):
            for c in range(n_col):
                to = (c // 2) * n_col + 2 * r + (m ^ (c & 1))
                pairs.append((r * n_col + c, to))
        return pairs

    def exchange(value, m):
        return lax.ppermute(value, ("row", "col"), swap_perm(m))

    def spread(row_part, col_part):
        own, other, down = [row_part], [], [col_part]
        for d in range(1, n_col // 2):
            own.append(xor_permute(row_part, "col", 2 * d, n_col))
        for e in range(1, n_row):
            down.append(xor_permute(col_part, "row", e, n_row))
        for d in range(n_col // 2):
            other.append(xor_permute(own[d], "col", 1, n_col))
        flat = []
        for d in range(n_col // 2):
            flat += [own[d], other[d]]
        return flat + down

    block = 2 * tile * SUBLANES

    def reduce_blocks(keep, send, cam, col_parts):
        got = xor_permute(send, "col", 1, n_col)
        cam = cam + xor_permute(cam, "col", 1, n_col)
        total = (keep + got).reshape(n_col // 2, block, LANES)
        col_total = col_parts[0]
        for e in range(1, n_row):
            col_total = col_total + xor_permute(col_parts[e], "row", e, n_row)
        row_total, cams = total[0], [cam]
        for d in range(1, n_col // 2):
            message = jnp.concatenate([total[d], cam], axis=0)
            message = xor_permute(message, "col", 2 * d, n_col)
            row_total = row_total + message[:block]
            cams.append(message[block:])
        cam_total = tree_sum(cams)
        row_total = row_total.reshape(2, tile, SUBLANES, LANES)
        col_total = col_total.reshape(2, tile, SUBLANES, LANES)
        return row_total, col_total, cam_total

    depth = log_depth.reshape(2, SUBLANES, tile, LANES).transpose(0, 2, 1, 3)
    depth = relative(depth)
    col_parts = [exchange(depth[m], m) for m in range(2)]
    col_depth = jnp.stack(col_parts)
    depths = spread(depth.reshape(-1, LANES), col_depth.reshape(-1, LANES))

    rates = [step_sizes[k : k + 1] for k in range(3)]
    camera_now, camera_state, camera_coef = update(camera_grads, 0, rates[1], camera.T, [], [])
    pair_now, pair_state, pair_coef = update(
        pair_grads, 0, rates[2], pair_pose.transpose(1, 2, 0), [], []
    )
    totals = None
    block_totals = []
    for step in range(1, ADAM_STEPS + 1):
        outs = grads_of_pairs(
            step,
            sizes,
            me,
            pair_coef,
            camera_coef,
            step_sizes,
            x,
            conf,
            table,
            (base, ray),
            depths,
            totals,
        )
        keep, send = outs[:2]
        col_parts = outs[2 : 2 + n_row]
        pair_sums, cam_sums = outs[2 + n_row :]
        row_total, col_total, cam_sums = reduce_blocks(keep, send, cam_sums, col_parts)
        if step < ADAM_STEPS:
            messages = [jnp.stack([row_total[m], col_total[m]]) for m in range(2)]
            received = [exchange(messages[m], m) for m in range(2)]
            total = row_total + jnp.stack([v[1] for v in received])
            col_total = col_total + jnp.stack([v[0] for v in received])
            message = jnp.concatenate([col_total.reshape(-1, LANES), cam_sums], axis=0)
            totals = spread(total.reshape(-1, LANES), message)
            cam_parts = totals[n_col:]
        else:
            received = [exchange(col_total[m], m) for m in range(2)]
            total = row_total + jnp.stack(received)
            others = [xor_permute(cam_sums, "row", e, n_row) for e in range(1, n_row)]
            cam_parts = [cam_sums, *others]
        block_totals.append(total)
        camera_now, camera_state, camera_coef = update(
            camera_grads, step, rates[1], camera_now, cam_parts, camera_state
        )
        pair_sums = jnp.sum(pair_sums, axis=-1).transpose(1, 2, 0)
        pair_now, pair_state, pair_coef = update(
            pair_grads, step, rates[2], pair_now, [pair_sums], pair_state
        )

    depth_now = depth
    depth_state = (jnp.zeros_like(depth),) * 2
    for step in range(1, ADAM_STEPS + 1):
        depth_now, *depth_state = adam_step(
            depth_now, block_totals[step - 1], *depth_state, step, step_sizes[0]
        )
    depth_now = relative(depth_now).transpose(0, 2, 1, 3).reshape(log_depth.shape)
    return depth_now, camera_now.T, pair_now.transpose(2, 0, 1)


def solution(mesh):
    n_row, n_col = mesh.shape["row"], mesh.shape["col"]
    in_specs = (
        P("row", "col", None, None, None),
        P("row", "col", None, None),
        P("row", "col", None),
        P("row", "col"),
        P(),
        P("row", "col", None),
        P(),
    )
    out_specs = (P("row", "col"), P(), P("row", "col", None))

    def body(pointmaps, *rest):
        rows, cols, pixels = pointmaps.shape[0], pointmaps.shape[1], pointmaps.shape[4]
        whole_tiles = pixels % (LANES * n_col) == 0 and (pixels // LANES) % SUBLANES == 0
        whole_tables = (rows * cols) % TABLE_PAIRS == 0
        paired = IMAGES <= LANES and rows == 2 * SUBLANES and cols == SUBLANES and n_col == 2 * n_row
        power = n_row & (n_row - 1) == 0
        if whole_tiles and whole_tables and paired and power:
            return fast_body(n_row, n_col, pointmaps, *rest)
        return general_body(pointmaps, *rest)

    return jax.shard_map(body, mesh=mesh, in_specs=in_specs, out_specs=out_specs, check_vma=False)
```

profile of v0, /device:TPU:12, one launch (start us, length us, event | category | flops | bytes accessed | tf_op | source)
XLA Modules:
  0.0 225.0 jit_solution(2683046393544351005)
XLA Ops:
  2.2 2.6 %collective-permute-start.3 = (f32[224,128]{1,0:T(8,128)S(1)}, f32[224,128]{1,0:T(8,128)S(1)}, u32[]{:S(2)}, u32[]{:S(2)}) collective-permute-start(f32[224,128]{1,0:T(8,128)S(1)} %bitcast.65), channel_id=1, source_target_pairs={{0,4},{1,5},{2,6},{3,7},{4,0},{5,1},{6,2},{7,3},{8,12},{9,13},{10,... | collective-permute-start | bytes 344072 | tf_op jit(solution)/shard_map/ppermute | solution.py:538
  5.3 4.4 %collective-permute-start.7 = (f32[14,8,128]{2,1,0:T(8,128)S(1)}, f32[14,8,128]{2,1,0:T(8,128)S(1)}, u32[]{:S(2)}, u32[]{:S(2)}) collective-permute-start(f32[14,8,128]{2,1,0:T(8,128)S(1)} %get-tuple-element.67), channel_id=1, source_target_pairs={{0,0},{1,1},{2,8},{3,9},{4,16},{5,17},{6,24},{7,25},{8,2},{9,3},{1... | collective-permute-start | bytes 172040 | tf_op jit(solution)/shard_map/ppermute | solution.py:583
  9.9 10.5 %collective-permute-done.7 = f32[14,8,128]{2,1,0:T(8,128)S(1)} collective-permute-done((f32[14,8,128]{2,1,0:T(8,128)S(1)}, f32[14,8,128]{2,1,0:T(8,128)S(1)}, u32[]{:S(2)}, u32[]{:S(2)}) %collective-permute-start.7) | collective-permute-done | bytes 57376 | tf_op jit(solution)/shard_map/ppermute | solution.py:583
  21.6 1.9 collective-permute-start.11
  23.4 1.7 collective-permute-start.9
  25.6 2.8 %collective-permute-done.10.refs_19_ = f32[224,128]{1,0:T(8,128)S(1)} collective-permute-done((f32[224,128]{1,0:T(8,128)S(1)}, f32[224,128]{1,0:T(8,128)S(1)}, u32[]{:S(2)}, u32[]{:S(2)}) %collective-permute-start.10) | collective-permute-done | bytes 114720 | tf_op jit(solution)/shard_map/ppermute | solution.py:538
  28.4 1.4 fusion.15
  35.1 47.7 %shard_map.123 = (f32[896,128]{1,0:T(8,128)}, f32[896,128]{1,0:T(8,128)}, f32[224,128]{1,0:T(8,128)S(1)}, f32[224,128]{1,0:T(8,128)S(1)}, f32[224,128]{1,0:T(8,1...) custom-call(s32[2]{0:T(128)S(1)} %pad_add_fusion.refs_0_, ...), custom_call_target="tpu_custom_call" | custom-call | flops 220200960 | bytes 33030144 | tf_op jit(solution)/shard_map/pallas_call | solution.py:394
  83.4 3.5 %collective-permute-start.19 = (f32[224,128]{1,0:T(8,128)S(1)}, f32[224,128]{1,0:T(8,128)S(1)}, u32[]{:S(2)}, u32[]{:S(2)}) collective-permute-start(f32[224,128]{1,0:T(8,128)S(1)} %get-tuple-element.33), channel_id=1, source_target_pairs={{0,24},{8,16},{16,8},{24,0},{1,25},{9,17},{17,9},{25,1},{2,26},{10... | collective-permute-start | bytes 344072 | tf_op jit(solution)/shard_map/ppermute | solution.py:538
  88.0 1.4 collective-permute-done.17
  89.4 1.6 collective-permute-done.18
  92.8 2.6 %collective-permute-start.15 = (f32[232,128]{1,0:T(8,128)S(1)}, f32[232,128]{1,0:T(8,128)S(1)}, u32[]{:S(2)}, u32[]{:S(2)}) collective-permute-start(f32[232,128]{1,0:T(8,128)S(1)} %get-tuple-element.73), channel_id=1, source_target_pairs={{0,4},{1,5},{2,6},{3,7},{4,0},{5,1},{6,2},{7,3},{8,12},{9,13},{10,... | collective-permute-start | bytes 356360 | tf_op jit(solution)/shard_map/ppermute | solution.py:538
  95.8 2.6 %collective-permute-done.14 = f32[232,128]{1,0:T(8,128)S(1)} collective-permute-done((f32[232,128]{1,0:T(8,128)S(1)}, f32[232,128]{1,0:T(8,128)S(1)}, u32[]{:S(2)}, u32[]{:S(2)}) %collective-permute-start.14) | collective-permute-done | bytes 118816 | tf_op jit(solution)/shard_map/ppermute | solution.py:538
  98.4 4.2 %collective-permute-done.15 = f32[232,128]{1,0:T(8,128)S(1)} collective-permute-done((f32[232,128]{1,0:T(8,128)S(1)}, f32[232,128]{1,0:T(8,128)S(1)}, u32[]{:S(2)}, u32[]{:S(2)}) %collective-permute-start.15) | collective-permute-done | bytes 118816 | tf_op jit(solution)/shard_map/ppermute | solution.py:538
  102.6 2.9 %collective-permute-done.16 = f32[232,128]{1,0:T(8,128)S(1)} collective-permute-done((f32[232,128]{1,0:T(8,128)S(1)}, f32[232,128]{1,0:T(8,128)S(1)}, u32[]{:S(2)}, u32[]{:S(2)}) %collective-permute-start.16) | collective-permute-done | bytes 118816 | tf_op jit(solution)/shard_map/ppermute | solution.py:538
  105.6 4.4 %collective-permute-start.20 = (f32[2,14,8,128]{3,2,1,0:T(8,128)S(1)}, f32[2,14,8,128]{3,2,1,0:T(8,128)S(1)}, u32[]{:S(2)}, u32[]{:S(2)}) collective-permute-start(f32[2,14,8,128]{3,2,1,0:T(8,128)S(1)} %pad_maximum_fusion.8), channel_id=1, source_target_pairs={{0,0},{1,1},{2,8},{3,9},{4,16},{5,17},{6,24},{7,25},{8,2},{9,3},{1... | collective-permute-start | bytes 344072 | tf_op jit(solution)/shard_map/ppermute | solution.py:583
  110.2 8.9 %collective-permute-done.20 = f32[2,14,8,128]{3,2,1,0:T(8,128)S(1)} collective-permute-done((f32[2,14,8,128]{3,2,1,0:T(8,128)S(1)}, f32[2,14,8,128]{3,2,1,0:T(8,128)S(1)}, u32[]{:S(2)}, u32[]{:S(2)}) %collective-permute-start.20) | collective-permute-done | bytes 114720 | tf_op jit(solution)/shard_map/ppermute | solution.py:583
  119.1 1.8 collective-permute-done.21
  121.2 5.7 %collective-permute-start.23 = (f32[232,128]{1,0:T(8,128)S(1)}, f32[232,128]{1,0:T(8,128)S(1)}, u32[]{:S(2)}, u32[]{:S(2)}) collective-permute-start(f32[232,128]{1,0:T(8,128)S(1)} %pad_maximum_fusion.6.refs_2_.refs_29_), channel_id=1, source_target_pairs={{0,16},{8,24},{16,0},{24,8},{1,17},{9,25},{17,1},{25,9},{2,18},{10... | collective-permute-start | bytes 356360 | tf_op jit(solution)/shard_map/ppermute | solution.py:538
  126.9 1.5 collective-permute-start.30
  128.3 1.3 collective-permute-start.24
  129.6 4.7 %collective-permute-done.28.refs_25_ = f32[224,128]{1,0:T(8,128)S(1)} collective-permute-done((f32[224,128]{1,0:T(8,128)S(1)}, f32[224,128]{1,0:T(8,128)S(1)}, u32[]{:S(2)}, u32[]{:S(2)}) %collective-permute-start.28) | collective-permute-done | bytes 114720 | tf_op jit(solution)/shard_map/ppermute | solution.py:538
  134.3 4.0 %collective-permute-done.30.refs_27_ = f32[224,128]{1,0:T(8,128)S(1)} collective-permute-done((f32[224,128]{1,0:T(8,128)S(1)}, f32[224,128]{1,0:T(8,128)S(1)}, u32[]{:S(2)}, u32[]{:S(2)}) %collective-permute-start.30) | collective-permute-done | bytes 114720 | tf_op jit(solution)/shard_map/ppermute | solution.py:538
  142.7 48.1 %shard_map.126 = (f32[896,128]{1,0:T(8,128)}, f32[896,128]{1,0:T(8,128)}, f32[224,128]{1,0:T(8,128)S(1)}, f32[224,128]{1,0:T(8,128)S(1)}, f32[224,128]{1,0:T(8,1...) custom-call(s32[2]{0:T(128)S(1)} %pad_add_fusion.refs_0_, ...), custom_call_target="tpu_custom_call" | custom-call | flops 220200960 | bytes 33030144 | tf_op jit(solution)/shard_map/pallas_call | solution.py:394
  192.8 2.0 collective-permute-start.39
  196.8 1.4 shard_map.128
  200.9 1.8 collective-permute-start.35
  203.7 3.8 %collective-permute-start.40 = (f32[14,8,128]{2,1,0:T(8,128)S(1)}, f32[14,8,128]{2,1,0:T(8,128)S(1)}, u32[]{:S(2)}, u32[]{:S(2)}) collective-permute-start(f32[14,8,128]{2,1,0:T(8,128)S(1)} %get-tuple-element.57), channel_id=1, source_target_pairs={{0,0},{1,1},{2,8},{3,9},{4,16},{5,17},{6,24},{7,25},{8,2},{9,3},{1... | collective-permute-start | bytes 172040 | tf_op jit(solution)/shard_map/ppermute | solution.py:583
  207.8 5.6 %collective-permute-done.35 = f32[232,128]{1,0:T(8,128)S(1)} collective-permute-done((f32[232,128]{1,0:T(8,128)S(1)}, f32[232,128]{1,0:T(8,128)S(1)}, u32[]{:S(2)}, u32[]{:S(2)}) %collective-permute-start.35) | collective-permute-done | bytes 118816 | tf_op jit(solution)/shard_map/ppermute | solution.py:538
  213.5 2.3 %collective-permute-done.36 = f32[232,128]{1,0:T(8,128)S(1)} collective-permute-done((f32[232,128]{1,0:T(8,128)S(1)}, f32[232,128]{1,0:T(8,128)S(1)}, u32[]{:S(2)}, u32[]{:S(2)}) %collective-permute-start.36) | collective-permute-done | bytes 118816 | tf_op jit(solution)/shard_map/ppermute | solution.py:538
  216.5 2.8 %collective-permute-start.43 = (f32[8,128]{1,0:T(8,128)S(1)}, f32[8,128]{1,0:T(8,128)S(1)}, u32[]{:S(2)}, u32[]{:S(2)}) collective-permute-start(f32[8,128]{1,0:T(8,128)S(1)} %fusion.9.refs_2_), channel_id=1, source_target_pairs={{0,16},{8,24},{16,0},{24,8},{1,17},{9,25},{17,1},{25,9},{2,18},{10... | collective-permute-start | bytes 12296 | tf_op jit(solution)/shard_map/ppermute | solution.py:538
  221.1 2.6 %collective-permute-done.44.refs_5_ = f32[8,128]{1,0:T(8,128)S(1)} collective-permute-done((f32[8,128]{1,0:T(8,128)S(1)}, f32[8,128]{1,0:T(8,128)S(1)}, u32[]{:S(2)}, u32[]{:S(2)}) %collective-permute-start.44) | collective-permute-done | bytes 4128 | tf_op jit(solution)/shard_map/ppermute | solution.py:538
  (156 shorter events, 28.7 us)
Async XLA Ops:
  1.7 19.9 %collective-permute-start.1 = (f32[224,128]{1,0:T(8,128)S(1)}, f32[224,128]{1,0:T(8,128)S(1)}, u32[]{:S(2)}, u32[]{:S(2)}) collective-permute-start(f32[224,128]{1,0:T(8,128)S(1)} %bitcast.64), channel_id=1, source_target_pairs={{0,2},{1,3},{2,0},{3,1},{4,6},{5,7},{6,4},{7,5},{8,10},{9,11},{10,... | collective-permute-start | bytes 344072 | tf_op jit(solution)/shard_map/ppermute | solution.py:538
  2.2 21.2 %collective-permute-start.3 = (f32[224,128]{1,0:T(8,128)S(1)}, f32[224,128]{1,0:T(8,128)S(1)}, u32[]{:S(2)}, u32[]{:S(2)}) collective-permute-start(f32[224,128]{1,0:T(8,128)S(1)} %bitcast.65), channel_id=1, source_target_pairs={{0,4},{1,5},{2,6},{3,7},{4,0},{5,1},{6,2},{7,3},{8,12},{9,13},{10,... | collective-permute-start | bytes 344072 | tf_op jit(solution)/shard_map/ppermute | solution.py:538
  4.8 20.3 %collective-permute-start.5 = (f32[224,128]{1,0:T(8,128)S(1)}, f32[224,128]{1,0:T(8,128)S(1)}, u32[]{:S(2)}, u32[]{:S(2)}) collective-permute-start(f32[224,128]{1,0:T(8,128)S(1)} %bitcast.66), channel_id=1, source_target_pairs={{0,6},{1,7},{2,4},{3,5},{4,2},{5,3},{6,0},{7,1},{8,14},{9,15},{10,... | collective-permute-start | bytes 344072 | tf_op jit(solution)/shard_map/ppermute | solution.py:538
  5.3 15.2 %collective-permute-start.7 = (f32[14,8,128]{2,1,0:T(8,128)S(1)}, f32[14,8,128]{2,1,0:T(8,128)S(1)}, u32[]{:S(2)}, u32[]{:S(2)}) collective-permute-start(f32[14,8,128]{2,1,0:T(8,128)S(1)} %get-tuple-element.67), channel_id=1, source_target_pairs={{0,0},{1,1},{2,8},{3,9},{4,16},{5,17},{6,24},{7,25},{8,2},{9,3},{1... | collective-permute-start | bytes 172040 | tf_op jit(solution)/shard_map/ppermute | solution.py:583
  9.6 10.8 %collective-permute-start.8 = (f32[14,8,128]{2,1,0:T(8,128)S(1)}, f32[14,8,128]{2,1,0:T(8,128)S(1)}, u32[]{:S(2)}, u32[]{:S(2)}) collective-permute-start(f32[14,8,128]{2,1,0:T(8,128)S(1)} %get-tuple-element.68), channel_id=1, source_target_pairs={{0,1},{1,0},{2,9},{3,8},{4,17},{5,16},{6,25},{7,24},{8,3},{9,2},{1... | collective-permute-start | bytes 172040 | tf_op jit(solution)/shard_map/ppermute | solution.py:583
  20.4 8.0 %collective-permute-start.10 = (f32[224,128]{1,0:T(8,128)S(1)}, f32[224,128]{1,0:T(8,128)S(1)}, u32[]{:S(2)}, u32[]{:S(2)}) collective-permute-start(f32[224,128]{1,0:T(8,128)S(1)} %bitcast.70), channel_id=1, source_target_pairs={{0,16},{8,24},{16,0},{24,8},{1,17},{9,25},{17,1},{25,9},{2,18},{10... | collective-permute-start | bytes 344072 | tf_op jit(solution)/shard_map/ppermute | solution.py:538
  21.6 11.4 %collective-permute-start.11 = (f32[224,128]{1,0:T(8,128)S(1)}, f32[224,128]{1,0:T(8,128)S(1)}, u32[]{:S(2)}, u32[]{:S(2)}) collective-permute-start(f32[224,128]{1,0:T(8,128)S(1)} %bitcast.71), channel_id=1, source_target_pairs={{0,24},{8,16},{16,8},{24,0},{1,25},{9,17},{17,9},{25,1},{2,26},{10... | collective-permute-start | bytes 344072 | tf_op jit(solution)/shard_map/ppermute | solution.py:538
  23.4 9.6 %collective-permute-start.9 = (f32[224,128]{1,0:T(8,128)S(1)}, f32[224,128]{1,0:T(8,128)S(1)}, u32[]{:S(2)}, u32[]{:S(2)}) collective-permute-start(f32[224,128]{1,0:T(8,128)S(1)} %bitcast.72), channel_id=1, source_target_pairs={{0,8},{8,0},{16,24},{24,16},{1,9},{9,1},{17,25},{25,17},{2,10},{10... | collective-permute-start | bytes 344072 | tf_op jit(solution)/shard_map/ppermute | solution.py:538
  25.1 7.9 %collective-permute-start.2 = (f32[224,128]{1,0:T(8,128)S(1)}, f32[224,128]{1,0:T(8,128)S(1)}, u32[]{:S(2)}, u32[]{:S(2)}) collective-permute-start(f32[224,128]{1,0:T(8,128)S(1)} %collective-permute-done.1.refs_11_), channel_id=1, source_target_pairs={{0,1},{1,0},{2,3},{3,2},{4,5},{5,4},{6,7},{7,6},{8,9},{9,8},{10,11... | collective-permute-start | bytes 344072 | tf_op jit(solution)/shard_map/ppermute | solution.py:538
  25.1 7.9 %collective-permute-start.4 = (f32[224,128]{1,0:T(8,128)S(1)}, f32[224,128]{1,0:T(8,128)S(1)}, u32[]{:S(2)}, u32[]{:S(2)}) collective-permute-start(f32[224,128]{1,0:T(8,128)S(1)} %collective-permute-done.3.refs_13_), channel_id=1, source_target_pairs={{0,1},{1,0},{2,3},{3,2},{4,5},{5,4},{6,7},{7,6},{8,9},{9,8},{10,11... | collective-permute-start | bytes 344072 | tf_op jit(solution)/shard_map/ppermute | solution.py:538
  82.8 8.3 %collective-permute-start.12 = (f32[896,128]{1,0:T(8,128)}, f32[896,128]{1,0:T(8,128)S(1)}, u32[]{:S(2)}, u32[]{:S(2)}) collective-permute-start(f32[896,128]{1,0:T(8,128)} %get-tuple-element.28), channel_id=1, source_target_pairs={{0,1},{1,0},{2,3},{3,2},{4,5},{5,4},{6,7},{7,6},{8,9},{9,8},{10,11... | collective-permute-start | bytes 1376264 | tf_op jit(solution)/shard_map/ppermute | solution.py:538
  83.4 7.7 %collective-permute-start.18 = (f32[224,128]{1,0:T(8,128)S(1)}, f32[224,128]{1,0:T(8,128)S(1)}, u32[]{:S(2)}, u32[]{:S(2)}) collective-permute-start(f32[224,128]{1,0:T(8,128)S(1)} %get-tuple-element.32), channel_id=1, source_target_pairs={{0,16},{8,24},{16,0},{24,8},{1,17},{9,25},{17,1},{25,9},{2,18},{10... | collective-permute-start | bytes 344072 | tf_op jit(solution)/shard_map/ppermute | solution.py:538
  83.4 7.7 %collective-permute-start.19 = (f32[224,128]{1,0:T(8,128)S(1)}, f32[224,128]{1,0:T(8,128)S(1)}, u32[]{:S(2)}, u32[]{:S(2)}) collective-permute-start(f32[224,128]{1,0:T(8,128)S(1)} %get-tuple-element.33), channel_id=1, source_target_pairs={{0,24},{8,16},{16,8},{24,0},{1,25},{9,17},{17,9},{25,1},{2,26},{10... | collective-permute-start | bytes 344072 | tf_op jit(solution)/shard_map/ppermute | solution.py:538
  92.8 9.8 %collective-permute-start.15 = (f32[232,128]{1,0:T(8,128)S(1)}, f32[232,128]{1,0:T(8,128)S(1)}, u32[]{:S(2)}, u32[]{:S(2)}) collective-permute-start(f32[232,128]{1,0:T(8,128)S(1)} %get-tuple-element.73), channel_id=1, source_target_pairs={{0,4},{1,5},{2,6},{3,7},{4,0},{5,1},{6,2},{7,3},{8,12},{9,13},{10,... | collective-permute-start | bytes 356360 | tf_op jit(solution)/shard_map/ppermute | solution.py:538
  95.4 10.1 %collective-permute-start.16 = (f32[232,128]{1,0:T(8,128)S(1)}, f32[232,128]{1,0:T(8,128)S(1)}, u32[]{:S(2)}, u32[]{:S(2)}) collective-permute-start(f32[232,128]{1,0:T(8,128)S(1)} %get-tuple-element.74), channel_id=1, source_target_pairs={{0,6},{1,7},{2,4},{3,5},{4,2},{5,3},{6,0},{7,1},{8,14},{9,15},{10,... | collective-permute-start | bytes 356360 | tf_op jit(solution)/shard_map/ppermute | solution.py:538
  105.6 13.5 %collective-permute-start.20 = (f32[2,14,8,128]{3,2,1,0:T(8,128)S(1)}, f32[2,14,8,128]{3,2,1,0:T(8,128)S(1)}, u32[]{:S(2)}, u32[]{:S(2)}) collective-permute-start(f32[2,14,8,128]{3,2,1,0:T(8,128)S(1)} %pad_maximum_fusion.8), channel_id=1, source_target_pairs={{0,0},{1,1},{2,8},{3,9},{4,16},{5,17},{6,24},{7,25},{8,2},{9,3},{1... | collective-permute-start | bytes 344072 | tf_op jit(solution)/shard_map/ppermute | solution.py:583
  110.1 10.8 %collective-permute-start.21 = (f32[2,14,8,128]{3,2,1,0:T(8,128)S(1)}, f32[2,14,8,128]{3,2,1,0:T(8,128)S(1)}, u32[]{:S(2)}, u32[]{:S(2)}) collective-permute-start(f32[2,14,8,128]{3,2,1,0:T(8,128)S(1)} %pad_maximum_fusion.9), channel_id=1, source_target_pairs={{0,1},{1,0},{2,9},{3,8},{4,17},{5,16},{6,25},{7,24},{8,3},{9,2},{1... | collective-permute-start | bytes 344072 | tf_op jit(solution)/shard_map/ppermute | solution.py:583
  121.0 7.4 %collective-permute-start.26 = (f32[224,128]{1,0:T(8,128)S(1)}, f32[224,128]{1,0:T(8,128)S(1)}, u32[]{:S(2)}, u32[]{:S(2)}) collective-permute-start(f32[224,128]{1,0:T(8,128)S(1)} %bitcast_add_fusion.refs_21_), channel_id=1, source_target_pairs={{0,2},{1,3},{2,0},{3,1},{4,6},{5,7},{6,4},{7,5},{8,10},{9,11},{10,... | collective-permute-start | bytes 344072 | tf_op jit(solution)/shard_map/ppermute | solution.py:538
  121.1 17.2 %collective-permute-start.22 = (f32[232,128]{1,0:T(8,128)S(1)}, f32[232,128]{1,0:T(8,128)S(1)}, u32[]{:S(2)}, u32[]{:S(2)}) collective-permute-start(f32[232,128]{1,0:T(8,128)S(1)} %pad_maximum_fusion.6.refs_2_.refs_29_), channel_id=1, source_target_pairs={{0,8},{8,0},{16,24},{24,16},{1,9},{9,1},{17,25},{25,17},{2,10},{10... | collective-permute-start | bytes 356360 | tf_op jit(solution)/shard_map/ppermute | solution.py:538
  121.2 17.6 %collective-permute-start.23 = (f32[232,128]{1,0:T(8,128)S(1)}, f32[232,128]{1,0:T(8,128)S(1)}, u32[]{:S(2)}, u32[]{:S(2)}) collective-permute-start(f32[232,128]{1,0:T(8,128)S(1)} %pad_maximum_fusion.6.refs_2_.refs_29_), channel_id=1, source_target_pairs={{0,16},{8,24},{16,0},{24,8},{1,17},{9,25},{17,1},{25,9},{2,18},{10... | collective-permute-start | bytes 356360 | tf_op jit(solution)/shard_map/ppermute | solution.py:538
  126.8 7.4 %collective-permute-start.28 = (f32[224,128]{1,0:T(8,128)S(1)}, f32[224,128]{1,0:T(8,128)S(1)}, u32[]{:S(2)}, u32[]{:S(2)}) collective-permute-start(f32[224,128]{1,0:T(8,128)S(1)} %bitcast_add_fusion.refs_21_), channel_id=1, source_target_pairs={{0,4},{1,5},{2,6},{3,7},{4,0},{5,1},{6,2},{7,3},{8,12},{9,13},{10,... | collective-permute-start | bytes 344072 | tf_op jit(solution)/shard_map/ppermute | solution.py:538
  126.9 11.5 %collective-permute-start.30 = (f32[224,128]{1,0:T(8,128)S(1)}, f32[224,128]{1,0:T(8,128)S(1)}, u32[]{:S(2)}, u32[]{:S(2)}) collective-permute-start(f32[224,128]{1,0:T(8,128)S(1)} %bitcast_add_fusion.refs_21_), channel_id=1, source_target_pairs={{0,6},{1,7},{2,4},{3,5},{4,2},{5,3},{6,0},{7,1},{8,14},{9,15},{10,... | collective-permute-start | bytes 344072 | tf_op jit(solution)/shard_map/ppermute | solution.py:538
  128.3 12.8 %collective-permute-start.24 = (f32[232,128]{1,0:T(8,128)S(1)}, f32[232,128]{1,0:T(8,128)S(1)}, u32[]{:S(2)}, u32[]{:S(2)}) collective-permute-start(f32[232,128]{1,0:T(8,128)S(1)} %pad_maximum_fusion.6.refs_2_.refs_29_), channel_id=1, source_target_pairs={{0,24},{8,16},{16,8},{24,0},{1,25},{9,17},{17,9},{25,1},{2,26},{10... | collective-permute-start | bytes 356360 | tf_op jit(solution)/shard_map/ppermute | solution.py:538
  134.3 7.6 %collective-permute-start.25 = (f32[224,128]{1,0:T(8,128)S(1)}, f32[224,128]{1,0:T(8,128)S(1)}, u32[]{:S(2)}, u32[]{:S(2)}) collective-permute-start(f32[224,128]{1,0:T(8,128)S(1)} %bitcast_add_fusion.refs_21_), channel_id=1, source_target_pairs={{0,1},{1,0},{2,3},{3,2},{4,5},{5,4},{6,7},{7,6},{8,9},{9,8},{10,11... | collective-permute-start | bytes 344072 | tf_op jit(solution)/shard_map/ppermute | solution.py:538
  190.8 8.2 %collective-permute-start.32 = (f32[896,128]{1,0:T(8,128)}, f32[896,128]{1,0:T(8,128)S(1)}, u32[]{:S(2)}, u32[]{:S(2)}) collective-permute-start(f32[896,128]{1,0:T(8,128)} %get-tuple-element.38), channel_id=1, source_target_pairs={{0,1},{1,0},{2,3},{3,2},{4,5},{5,4},{6,7},{7,6},{8,9},{9,8},{10,11... | collective-permute-start | bytes 1376264 | tf_op jit(solution)/shard_map/ppermute | solution.py:538
  191.3 7.0 %collective-permute-start.37 = (f32[224,128]{1,0:T(8,128)S(1)}, f32[224,128]{1,0:T(8,128)S(1)}, u32[]{:S(2)}, u32[]{:S(2)}) collective-permute-start(f32[224,128]{1,0:T(8,128)S(1)} %get-tuple-element.41), channel_id=1, source_target_pairs={{0,8},{8,0},{16,24},{24,16},{1,9},{9,1},{17,25},{25,17},{2,10},{10... | collective-permute-start | bytes 344072 | tf_op jit(solution)/shard_map/ppermute | solution.py:538
  191.7 7.3 %collective-permute-start.38 = (f32[224,128]{1,0:T(8,128)S(1)}, f32[224,128]{1,0:T(8,128)S(1)}, u32[]{:S(2)}, u32[]{:S(2)}) collective-permute-start(f32[224,128]{1,0:T(8,128)S(1)} %get-tuple-element.42), channel_id=1, source_target_pairs={{0,16},{8,24},{16,0},{24,8},{1,17},{9,25},{17,1},{25,9},{2,18},{10... | collective-permute-start | bytes 344072 | tf_op jit(solution)/shard_map/ppermute | solution.py:538
  200.2 7.7 %collective-permute-start.34 = (f32[232,128]{1,0:T(8,128)S(1)}, f32[232,128]{1,0:T(8,128)S(1)}, u32[]{:S(2)}, u32[]{:S(2)}) collective-permute-start(f32[232,128]{1,0:T(8,128)S(1)} %get-tuple-element.69), channel_id=1, source_target_pairs={{0,2},{1,3},{2,0},{3,1},{4,6},{5,7},{6,4},{7,5},{8,10},{9,11},{10,... | collective-permute-start | bytes 356360 | tf_op jit(solution)/shard_map/ppermute | solution.py:538
  200.9 12.6 %collective-permute-start.35 = (f32[232,128]{1,0:T(8,128)S(1)}, f32[232,128]{1,0:T(8,128)S(1)}, u32[]{:S(2)}, u32[]{:S(2)}) collective-permute-start(f32[232,128]{1,0:T(8,128)S(1)} %get-tuple-element.70), channel_id=1, source_target_pairs={{0,4},{1,5},{2,6},{3,7},{4,0},{5,1},{6,2},{7,3},{8,12},{9,13},{10,... | collective-permute-start | bytes 356360 | tf_op jit(solution)/shard_map/ppermute | solution.py:538
  202.7 13.1 %collective-permute-start.36 = (f32[232,128]{1,0:T(8,128)S(1)}, f32[232,128]{1,0:T(8,128)S(1)}, u32[]{:S(2)}, u32[]{:S(2)}) collective-permute-start(f32[232,128]{1,0:T(8,128)S(1)} %get-tuple-element.71), channel_id=1, source_target_pairs={{0,6},{1,7},{2,4},{3,5},{4,2},{5,3},{6,0},{7,1},{8,14},{9,15},{10,... | collective-permute-start | bytes 356360 | tf_op jit(solution)/shard_map/ppermute | solution.py:538
  203.7 15.9 %collective-permute-start.40 = (f32[14,8,128]{2,1,0:T(8,128)S(1)}, f32[14,8,128]{2,1,0:T(8,128)S(1)}, u32[]{:S(2)}, u32[]{:S(2)}) collective-permute-start(f32[14,8,128]{2,1,0:T(8,128)S(1)} %get-tuple-element.57), channel_id=1, source_target_pairs={{0,0},{1,1},{2,8},{3,9},{4,16},{5,17},{6,24},{7,25},{8,2},{9,3},{1... | collective-permute-start | bytes 172040 | tf_op jit(solution)/shard_map/ppermute | solution.py:583
  207.5 12.1 %collective-permute-start.41 = (f32[14,8,128]{2,1,0:T(8,128)S(1)}, f32[14,8,128]{2,1,0:T(8,128)S(1)}, u32[]{:S(2)}, u32[]{:S(2)}) collective-permute-start(f32[14,8,128]{2,1,0:T(8,128)S(1)} %get-tuple-element.58), channel_id=1, source_target_pairs={{0,1},{1,0},{2,9},{3,8},{4,17},{5,16},{6,25},{7,24},{8,3},{9,2},{1... | collective-permute-start | bytes 172040 | tf_op jit(solution)/shard_map/ppermute | solution.py:583
  (35 other events, 835.2 us)
where the time goes:
time: 226 us; the launch traced here: 225 us
  Pallas kernels  101 us (45%)
  waiting for transfers between devices  58 us (26%)
  starting transfers between devices  48.8 us (22%)
  other arithmetic  7.59 us (3%)
  local copies, waits for them, and re-layouts  6.39 us (3%)
    pallas_call x2, Pallas kernels, grads_of_pairs(): pl.pallas_call(functools.partial(grad_kernel, sizes, step), grid=(rows,),...  95.7 us
    ppermute x39, waiting for transfers between devices, xor_permute(): return lax.ppermute(value, axis, [(c, c ^ bit) for c in range(size)])  36.8 us
    ppermute x39, starting transfers between devices, xor_permute(): return lax.ppermute(value, axis, [(c, c ^ bit) for c in range(size)])  35.7 us
    ppermute x6, waiting for transfers between devices, exchange(): return lax.ppermute(value, ('row', 'col'), swap_perm(m))  21.2 us
    ppermute x6, starting transfers between devices, exchange(): return lax.ppermute(value, ('row', 'col'), swap_perm(m))  13.1 us
    pallas_call x6, Pallas kernels, update(): outs = outs(rate, *operands)  5.5 us
  transfers between devices with their start and end apart: 45, of which 16 were waited for; matrix products, arithmetic and copies ran while one was open for 3% of the time, Pallas kernels for 2%

commit v1 on v0

--- a/solution.py
+++ b/solution.py
@@ -602,8 +602,9 @@
         cam = cam + xor_permute(cam, "col", 1, n_col)
         total = (keep + got).reshape(n_col // 2, block, LANES)
         col_total = col_parts[0]
-        for e in range(1, n_row):
-            col_total = col_total + xor_permute(col_parts[e], "row", e, n_row)
+        got = [xor_permute(col_parts[e], "row", e, n_row) for e in range(1, n_row)]
+        for part in got:
+            col_total = col_total + part
         row_total, cams = total[0], [cam]
         for d in range(1, n_col // 2):
             message = jnp.concatenate([total[d], cam], axis=0)

time: 226 us -> 226 us (level)
  no operation moved by 1% of the time
where the time goes in v1:
time: 226 us; the launch traced here: 225 us
  Pallas kernels  101 us (45%)
  waiting for transfers between devices  58 us (26%)
  starting transfers between devices  48.8 us (22%)
  other arithmetic  7.59 us (3%)
  local copies, waits for them, and re-layouts  6.39 us (3%)
    pallas_call x2, Pallas kernels, grads_of_pairs(): pl.pallas_call(functools.partial(grad_kernel, sizes, step), grid=(rows,),...  95.7 us
    ppermute x39, waiting for transfers between devices, xor_permute(): return lax.ppermute(value, axis, [(c, c ^ bit) for c in range(size)])  36.8 us
    ppermute x39, starting transfers between devices, xor_permute(): return lax.ppermute(value, axis, [(c, c ^ bit) for c in range(size)])  35.7 us
    ppermute x6, waiting for transfers between devices, exchange(): return lax.ppermute(value, ('row', 'col'), swap_perm(m))  21.2 us
    ppermute x6, starting transfers between devices, exchange(): return lax.ppermute(value, ('row', 'col'), swap_perm(m))  13.1 us
    pallas_call x6, Pallas kernels, update(): outs = outs(rate, *operands)  5.5 us
  transfers between devices with their start and end apart: 45, of which 16 were waited for; matrix products, arithmetic and copies ran while one was open for 3% of the time, Pallas kernels for 2%

profile of v1, /device:TPU:12, one launch (start us, length us, event | category | flops | bytes accessed | tf_op | source)
XLA Modules:
  0.0 225.0 jit_solution(2683046393544351005)
XLA Ops:
  2.2 2.6 %collective-permute-start.3 = (f32[224,128]{1,0:T(8,128)S(1)}, f32[224,128]{1,0:T(8,128)S(1)}, u32[]{:S(2)}, u32[]{:S(2)}) collective-permute-start(f32[224,128]{1,0:T(8,128)S(1)} %bitcast.65), channel_id=1, source_target_pairs={{0,4},{1,5},{2,6},{3,7},{4,0},{5,1},{6,2},{7,3},{8,12},{9,13},{10,... | collective-permute-start | bytes 344072 | tf_op jit(solution)/shard_map/ppermute | solution.py:538
  5.3 4.4 %collective-permute-start.7 = (f32[14,8,128]{2,1,0:T(8,128)S(1)}, f32[14,8,128]{2,1,0:T(8,128)S(1)}, u32[]{:S(2)}, u32[]{:S(2)}) collective-permute-start(f32[14,8,128]{2,1,0:T(8,128)S(1)} %get-tuple-element.67), channel_id=1, source_target_pairs={{0,0},{1,1},{2,8},{3,9},{4,16},{5,17},{6,24},{7,25},{8,2},{9,3},{1... | collective-permute-start | bytes 172040 | tf_op jit(solution)/shard_map/ppermute | solution.py:583
  9.9 10.5 %collective-permute-done.7 = f32[14,8,128]{2,1,0:T(8,128)S(1)} collective-permute-done((f32[14,8,128]{2,1,0:T(8,128)S(1)}, f32[14,8,128]{2,1,0:T(8,128)S(1)}, u32[]{:S(2)}, u32[]{:S(2)}) %collective-permute-start.7) | collective-permute-done | bytes 57376 | tf_op jit(solution)/shard_map/ppermute | solution.py:583
  21.6 1.9 collective-permute-start.11
  23.4 1.7 collective-permute-start.9
  25.6 2.8 %collective-permute-done.10.refs_19_ = f32[224,128]{1,0:T(8,128)S(1)} collective-permute-done((f32[224,128]{1,0:T(8,128)S(1)}, f32[224,128]{1,0:T(8,128)S(1)}, u32[]{:S(2)}, u32[]{:S(2)}) %collective-permute-start.10) | collective-permute-done | bytes 114720 | tf_op jit(solution)/shard_map/ppermute | solution.py:538
  28.4 1.4 fusion.15
  35.1 47.7 %shard_map.123 = (f32[896,128]{1,0:T(8,128)}, f32[896,128]{1,0:T(8,128)}, f32[224,128]{1,0:T(8,128)S(1)}, f32[224,128]{1,0:T(8,128)S(1)}, f32[224,128]{1,0:T(8,1...) custom-call(s32[2]{0:T(128)S(1)} %pad_add_fusion.refs_0_, ...), custom_call_target="tpu_custom_call" | custom-call | flops 220200960 | bytes 33030144 | tf_op jit(solution)/shard_map/pallas_call | solution.py:394
  83.4 3.5 %collective-permute-start.19 = (f32[224,128]{1,0:T(8,128)S(1)}, f32[224,128]{1,0:T(8,128)S(1)}, u32[]{:S(2)}, u32[]{:S(2)}) collective-permute-start(f32[224,128]{1,0:T(8,128)S(1)} %get-tuple-element.33), channel_id=1, source_target_pairs={{0,24},{8,16},{16,8},{24,0},{1,25},{9,17},{17,9},{25,1},{2,26},{10... | collective-permute-start | bytes 344072 | tf_op jit(solution)/shard_map/ppermute | solution.py:538
  88.0 1.4 collective-permute-done.17
  89.4 1.6 collective-permute-done.18
  92.8 2.6 %collective-permute-start.15 = (f32[232,128]{1,0:T(8,128)S(1)}, f32[232,128]{1,0:T(8,128)S(1)}, u32[]{:S(2)}, u32[]{:S(2)}) collective-permute-start(f32[232,128]{1,0:T(8,128)S(1)} %get-tuple-element.73), channel_id=1, source_target_pairs={{0,4},{1,5},{2,6},{3,7},{4,0},{5,1},{6,2},{7,3},{8,12},{9,13},{10,... | collective-permute-start | bytes 356360 | tf_op jit(solution)/shard_map/ppermute | solution.py:538
  95.8 2.6 %collective-permute-done.14 = f32[232,128]{1,0:T(8,128)S(1)} collective-permute-done((f32[232,128]{1,0:T(8,128)S(1)}, f32[232,128]{1,0:T(8,128)S(1)}, u32[]{:S(2)}, u32[]{:S(2)}) %collective-permute-start.14) | collective-permute-done | bytes 118816 | tf_op jit(solution)/shard_map/ppermute | solution.py:538
  98.4 4.2 %collective-permute-done.15 = f32[232,128]{1,0:T(8,128)S(1)} collective-permute-done((f32[232,128]{1,0:T(8,128)S(1)}, f32[232,128]{1,0:T(8,128)S(1)}, u32[]{:S(2)}, u32[]{:S(2)}) %collective-permute-start.15) | collective-permute-done | bytes 118816 | tf_op jit(solution)/shard_map/ppermute | solution.py:538
  102.6 2.9 %collective-permute-done.16 = f32[232,128]{1,0:T(8,128)S(1)} collective-permute-done((f32[232,128]{1,0:T(8,128)S(1)}, f32[232,128]{1,0:T(8,128)S(1)}, u32[]{:S(2)}, u32[]{:S(2)}) %collective-permute-start.16) | collective-permute-done | bytes 118816 | tf_op jit(solution)/shard_map/ppermute | solution.py:538
  105.6 4.4 %collective-permute-start.20 = (f32[2,14,8,128]{3,2,1,0:T(8,128)S(1)}, f32[2,14,8,128]{3,2,1,0:T(8,128)S(1)}, u32[]{:S(2)}, u32[]{:S(2)}) collective-permute-start(f32[2,14,8,128]{3,2,1,0:T(8,128)S(1)} %pad_maximum_fusion.8), channel_id=1, source_target_pairs={{0,0},{1,1},{2,8},{3,9},{4,16},{5,17},{6,24},{7,25},{8,2},{9,3},{1... | collective-permute-start | bytes 344072 | tf_op jit(solution)/shard_map/ppermute | solution.py:583
  110.2 8.9 %collective-permute-done.20 = f32[2,14,8,128]{3,2,1,0:T(8,128)S(1)} collective-permute-done((f32[2,14,8,128]{3,2,1,0:T(8,128)S(1)}, f32[2,14,8,128]{3,2,1,0:T(8,128)S(1)}, u32[]{:S(2)}, u32[]{:S(2)}) %collective-permute-start.20) | collective-permute-done | bytes 114720 | tf_op jit(solution)/shard_map/ppermute | solution.py:583
  119.1 1.8 collective-permute-done.21
  121.2 5.7 %collective-permute-start.23 = (f32[232,128]{1,0:T(8,128)S(1)}, f32[232,128]{1,0:T(8,128)S(1)}, u32[]{:S(2)}, u32[]{:S(2)}) collective-permute-start(f32[232,128]{1,0:T(8,128)S(1)} %pad_maximum_fusion.6.refs_2_.refs_29_), channel_id=1, source_target_pairs={{0,16},{8,24},{16,0},{24,8},{1,17},{9,25},{17,1},{25,9},{2,18},{10... | collective-permute-start | bytes 356360 | tf_op jit(solution)/shard_map/ppermute | solution.py:538
  126.9 1.5 collective-permute-start.30
  128.3 1.3 collective-permute-start.24
  129.6 4.7 %collective-permute-done.28.refs_25_ = f32[224,128]{1,0:T(8,128)S(1)} collective-permute-done((f32[224,128]{1,0:T(8,128)S(1)}, f32[224,128]{1,0:T(8,128)S(1)}, u32[]{:S(2)}, u32[]{:S(2)}) %collective-permute-start.28) | collective-permute-done | bytes 114720 | tf_op jit(solution)/shard_map/ppermute | solution.py:538
  134.3 4.0 %collective-permute-done.30.refs_27_ = f32[224,128]{1,0:T(8,128)S(1)} collective-permute-done((f32[224,128]{1,0:T(8,128)S(1)}, f32[224,128]{1,0:T(8,128)S(1)}, u32[]{:S(2)}, u32[]{:S(2)}) %collective-permute-start.30) | collective-permute-done | bytes 114720 | tf_op jit(solution)/shard_map/ppermute | solution.py:538
  142.7 48.1 %shard_map.126 = (f32[896,128]{1,0:T(8,128)}, f32[896,128]{1,0:T(8,128)}, f32[224,128]{1,0:T(8,128)S(1)}, f32[224,128]{1,0:T(8,128)S(1)}, f32[224,128]{1,0:T(8,1...) custom-call(s32[2]{0:T(128)S(1)} %pad_add_fusion.refs_0_, ...), custom_call_target="tpu_custom_call" | custom-call | flops 220200960 | bytes 33030144 | tf_op jit(solution)/shard_map/pallas_call | solution.py:394
  192.8 2.0 collective-permute-start.39
  196.8 1.4 shard_map.128
  200.9 1.8 collective-permute-start.35
  203.7 3.8 %collective-permute-start.40 = (f32[14,8,128]{2,1,0:T(8,128)S(1)}, f32[14,8,128]{2,1,0:T(8,128)S(1)}, u32[]{:S(2)}, u32[]{:S(2)}) collective-permute-start(f32[14,8,128]{2,1,0:T(8,128)S(1)} %get-tuple-element.57), channel_id=1, source_target_pairs={{0,0},{1,1},{2,8},{3,9},{4,16},{5,17},{6,24},{7,25},{8,2},{9,3},{1... | collective-permute-start | bytes 172040 | tf_op jit(solution)/shard_map/ppermute | solution.py:583
  207.8 5.6 %collective-permute-done.35 = f32[232,128]{1,0:T(8,128)S(1)} collective-permute-done((f32[232,128]{1,0:T(8,128)S(1)}, f32[232,128]{1,0:T(8,128)S(1)}, u32[]{:S(2)}, u32[]{:S(2)}) %collective-permute-start.35) | collective-permute-done | bytes 118816 | tf_op jit(solution)/shard_map/ppermute | solution.py:538
  213.5 2.3 %collective-permute-done.36 = f32[232,128]{1,0:T(8,128)S(1)} collective-permute-done((f32[232,128]{1,0:T(8,128)S(1)}, f32[232,128]{1,0:T(8,128)S(1)}, u32[]{:S(2)}, u32[]{:S(2)}) %collective-permute-start.36) | collective-permute-done | bytes 118816 | tf_op jit(solution)/shard_map/ppermute | solution.py:538
  216.5 2.8 %collective-permute-start.43 = (f32[8,128]{1,0:T(8,128)S(1)}, f32[8,128]{1,0:T(8,128)S(1)}, u32[]{:S(2)}, u32[]{:S(2)}) collective-permute-start(f32[8,128]{1,0:T(8,128)S(1)} %fusion.9.refs_2_), channel_id=1, source_target_pairs={{0,16},{8,24},{16,0},{24,8},{1,17},{9,25},{17,1},{25,9},{2,18},{10... | collective-permute-start | bytes 12296 | tf_op jit(solution)/shard_map/ppermute | solution.py:538
  221.1 2.6 %collective-permute-done.44.refs_5_ = f32[8,128]{1,0:T(8,128)S(1)} collective-permute-done((f32[8,128]{1,0:T(8,128)S(1)}, f32[8,128]{1,0:T(8,128)S(1)}, u32[]{:S(2)}, u32[]{:S(2)}) %collective-permute-start.44) | collective-permute-done | bytes 4128 | tf_op jit(solution)/shard_map/ppermute | solution.py:538
  (156 shorter events, 28.7 us)
Async XLA Ops:
  1.7 19.9 %collective-permute-start.1 = (f32[224,128]{1,0:T(8,128)S(1)}, f32[224,128]{1,0:T(8,128)S(1)}, u32[]{:S(2)}, u32[]{:S(2)}) collective-permute-start(f32[224,128]{1,0:T(8,128)S(1)} %bitcast.64), channel_id=1, source_target_pairs={{0,2},{1,3},{2,0},{3,1},{4,6},{5,7},{6,4},{7,5},{8,10},{9,11},{10,... | collective-permute-start | bytes 344072 | tf_op jit(solution)/shard_map/ppermute | solution.py:538
  2.2 21.2 %collective-permute-start.3 = (f32[224,128]{1,0:T(8,128)S(1)}, f32[224,128]{1,0:T(8,128)S(1)}, u32[]{:S(2)}, u32[]{:S(2)}) collective-permute-start(f32[224,128]{1,0:T(8,128)S(1)} %bitcast.65), channel_id=1, source_target_pairs={{0,4},{1,5},{2,6},{3,7},{4,0},{5,1},{6,2},{7,3},{8,12},{9,13},{10,... | collective-permute-start | bytes 344072 | tf_op jit(solution)/shard_map/ppermute | solution.py:538
  4.8 20.3 %collective-permute-start.5 = (f32[224,128]{1,0:T(8,128)S(1)}, f32[224,128]{1,0:T(8,128)S(1)}, u32[]{:S(2)}, u32[]{:S(2)}) collective-permute-start(f32[224,128]{1,0:T(8,128)S(1)} %bitcast.66), channel_id=1, source_target_pairs={{0,6},{1,7},{2,4},{3,5},{4,2},{5,3},{6,0},{7,1},{8,14},{9,15},{10,... | collective-permute-start | bytes 344072 | tf_op jit(solution)/shard_map/ppermute | solution.py:538
  5.3 15.2 %collective-permute-start.7 = (f32[14,8,128]{2,1,0:T(8,128)S(1)}, f32[14,8,128]{2,1,0:T(8,128)S(1)}, u32[]{:S(2)}, u32[]{:S(2)}) collective-permute-start(f32[14,8,128]{2,1,0:T(8,128)S(1)} %get-tuple-element.67), channel_id=1, source_target_pairs={{0,0},{1,1},{2,8},{3,9},{4,16},{5,17},{6,24},{7,25},{8,2},{9,3},{1... | collective-permute-start | bytes 172040 | tf_op jit(solution)/shard_map/ppermute | solution.py:583
  9.6 10.8 %collective-permute-start.8 = (f32[14,8,128]{2,1,0:T(8,128)S(1)}, f32[14,8,128]{2,1,0:T(8,128)S(1)}, u32[]{:S(2)}, u32[]{:S(2)}) collective-permute-start(f32[14,8,128]{2,1,0:T(8,128)S(1)} %get-tuple-element.68), channel_id=1, source_target_pairs={{0,1},{1,0},{2,9},{3,8},{4,17},{5,16},{6,25},{7,24},{8,3},{9,2},{1... | collective-permute-start | bytes 172040 | tf_op jit(solution)/shard_map/ppermute | solution.py:583
  20.4 8.0 %collective-permute-start.10 = (f32[224,128]{1,0:T(8,128)S(1)}, f32[224,128]{1,0:T(8,128)S(1)}, u32[]{:S(2)}, u32[]{:S(2)}) collective-permute-start(f32[224,128]{1,0:T(8,128)S(1)} %bitcast.70), channel_id=1, source_target_pairs={{0,16},{8,24},{16,0},{24,8},{1,17},{9,25},{17,1},{25,9},{2,18},{10... | collective-permute-start | bytes 344072 | tf_op jit(solution)/shard_map/ppermute | solution.py:538
  21.6 11.4 %collective-permute-start.11 = (f32[224,128]{1,0:T(8,128)S(1)}, f32[224,128]{1,0:T(8,128)S(1)}, u32[]{:S(2)}, u32[]{:S(2)}) collective-permute-start(f32[224,128]{1,0:T(8,128)S(1)} %bitcast.71), channel_id=1, source_target_pairs={{0,24},{8,16},{16,8},{24,0},{1,25},{9,17},{17,9},{25,1},{2,26},{10... | collective-permute-start | bytes 344072 | tf_op jit(solution)/shard_map/ppermute | solution.py:538
  23.4 9.6 %collective-permute-start.9 = (f32[224,128]{1,0:T(8,128)S(1)}, f32[224,128]{1,0:T(8,128)S(1)}, u32[]{:S(2)}, u32[]{:S(2)}) collective-permute-start(f32[224,128]{1,0:T(8,128)S(1)} %bitcast.72), channel_id=1, source_target_pairs={{0,8},{8,0},{16,24},{24,16},{1,9},{9,1},{17,25},{25,17},{2,10},{10... | collective-permute-start | bytes 344072 | tf_op jit(solution)/shard_map/ppermute | solution.py:538
  25.1 7.9 %collective-permute-start.2 = (f32[224,128]{1,0:T(8,128)S(1)}, f32[224,128]{1,0:T(8,128)S(1)}, u32[]{:S(2)}, u32[]{:S(2)}) collective-permute-start(f32[224,128]{1,0:T(8,128)S(1)} %collective-permute-done.1.refs_11_), channel_id=1, source_target_pairs={{0,1},{1,0},{2,3},{3,2},{4,5},{5,4},{6,7},{7,6},{8,9},{9,8},{10,11... | collective-permute-start | bytes 344072 | tf_op jit(solution)/shard_map/ppermute | solution.py:538
  25.1 7.9 %collective-permute-start.4 = (f32[224,128]{1,0:T(8,128)S(1)}, f32[224,128]{1,0:T(8,128)S(1)}, u32[]{:S(2)}, u32[]{:S(2)}) collective-permute-start(f32[224,128]{1,0:T(8,128)S(1)} %collective-permute-done.3.refs_13_), channel_id=1, source_target_pairs={{0,1},{1,0},{2,3},{3,2},{4,5},{5,4},{6,7},{7,6},{8,9},{9,8},{10,11... | collective-permute-start | bytes 344072 | tf_op jit(solution)/shard_map/ppermute | solution.py:538
  82.8 8.3 %collective-permute-start.12 = (f32[896,128]{1,0:T(8,128)}, f32[896,128]{1,0:T(8,128)S(1)}, u32[]{:S(2)}, u32[]{:S(2)}) collective-permute-start(f32[896,128]{1,0:T(8,128)} %get-tuple-element.28), channel_id=1, source_target_pairs={{0,1},{1,0},{2,3},{3,2},{4,5},{5,4},{6,7},{7,6},{8,9},{9,8},{10,11... | collective-permute-start | bytes 1376264 | tf_op jit(solution)/shard_map/ppermute | solution.py:538
  83.4 7.7 %collective-permute-start.18 = (f32[224,128]{1,0:T(8,128)S(1)}, f32[224,128]{1,0:T(8,128)S(1)}, u32[]{:S(2)}, u32[]{:S(2)}) collective-permute-start(f32[224,128]{1,0:T(8,128)S(1)} %get-tuple-element.32), channel_id=1, source_target_pairs={{0,16},{8,24},{16,0},{24,8},{1,17},{9,25},{17,1},{25,9},{2,18},{10... | collective-permute-start | bytes 344072 | tf_op jit(solution)/shard_map/ppermute | solution.py:538
  83.4 7.7 %collective-permute-start.19 = (f32[224,128]{1,0:T(8,128)S(1)}, f32[224,128]{1,0:T(8,128)S(1)}, u32[]{:S(2)}, u32[]{:S(2)}) collective-permute-start(f32[224,128]{1,0:T(8,128)S(1)} %get-tuple-element.33), channel_id=1, source_target_pairs={{0,24},{8,16},{16,8},{24,0},{1,25},{9,17},{17,9},{25,1},{2,26},{10... | collective-permute-start | bytes 344072 | tf_op jit(solution)/shard_map/ppermute | solution.py:538
  92.8 9.8 %collective-permute-start.15 = (f32[232,128]{1,0:T(8,128)S(1)}, f32[232,128]{1,0:T(8,128)S(1)}, u32[]{:S(2)}, u32[]{:S(2)}) collective-permute-start(f32[232,128]{1,0:T(8,128)S(1)} %get-tuple-element.73), channel_id=1, source_target_pairs={{0,4},{1,5},{2,6},{3,7},{4,0},{5,1},{6,2},{7,3},{8,12},{9,13},{10,... | collective-permute-start | bytes 356360 | tf_op jit(solution)/shard_map/ppermute | solution.py:538
  95.4 10.1 %collective-permute-start.16 = (f32[232,128]{1,0:T(8,128)S(1)}, f32[232,128]{1,0:T(8,128)S(1)}, u32[]{:S(2)}, u32[]{:S(2)}) collective-permute-start(f32[232,128]{1,0:T(8,128)S(1)} %get-tuple-element.74), channel_id=1, source_target_pairs={{0,6},{1,7},{2,4},{3,5},{4,2},{5,3},{6,0},{7,1},{8,14},{9,15},{10,... | collective-permute-start | bytes 356360 | tf_op jit(solution)/shard_map/ppermute | solution.py:538
  105.6 13.5 %collective-permute-start.20 = (f32[2,14,8,128]{3,2,1,0:T(8,128)S(1)}, f32[2,14,8,128]{3,2,1,0:T(8,128)S(1)}, u32[]{:S(2)}, u32[]{:S(2)}) collective-permute-start(f32[2,14,8,128]{3,2,1,0:T(8,128)S(1)} %pad_maximum_fusion.8), channel_id=1, source_target_pairs={{0,0},{1,1},{2,8},{3,9},{4,16},{5,17},{6,24},{7,25},{8,2},{9,3},{1... | collective-permute-start | bytes 344072 | tf_op jit(solution)/shard_map/ppermute | solution.py:583
  110.1 10.8 %collective-permute-start.21 = (f32[2,14,8,128]{3,2,1,0:T(8,128)S(1)}, f32[2,14,8,128]{3,2,1,0:T(8,128)S(1)}, u32[]{:S(2)}, u32[]{:S(2)}) collective-permute-start(f32[2,14,8,128]{3,2,1,0:T(8,128)S(1)} %pad_maximum_fusion.9), channel_id=1, source_target_pairs={{0,1},{1,0},{2,9},{3,8},{4,17},{5,16},{6,25},{7,24},{8,3},{9,2},{1... | collective-permute-start | bytes 344072 | tf_op jit(solution)/shard_map/ppermute | solution.py:583
  121.0 7.4 %collective-permute-start.26 = (f32[224,128]{1,0:T(8,128)S(1)}, f32[224,128]{1,0:T(8,128)S(1)}, u32[]{:S(2)}, u32[]{:S(2)}) collective-permute-start(f32[224,128]{1,0:T(8,128)S(1)} %bitcast_add_fusion.refs_21_), channel_id=1, source_target_pairs={{0,2},{1,3},{2,0},{3,1},{4,6},{5,7},{6,4},{7,5},{8,10},{9,11},{10,... | collective-permute-start | bytes 344072 | tf_op jit(solution)/shard_map/ppermute | solution.py:538
  121.1 17.2 %collective-permute-start.22 = (f32[232,128]{1,0:T(8,128)S(1)}, f32[232,128]{1,0:T(8,128)S(1)}, u32[]{:S(2)}, u32[]{:S(2)}) collective-permute-start(f32[232,128]{1,0:T(8,128)S(1)} %pad_maximum_fusion.6.refs_2_.refs_29_), channel_id=1, source_target_pairs={{0,8},{8,0},{16,24},{24,16},{1,9},{9,1},{17,25},{25,17},{2,10},{10... | collective-permute-start | bytes 356360 | tf_op jit(solution)/shard_map/ppermute | solution.py:538
  121.2 17.6 %collective-permute-start.23 = (f32[232,128]{1,0:T(8,128)S(1)}, f32[232,128]{1,0:T(8,128)S(1)}, u32[]{:S(2)}, u32[]{:S(2)}) collective-permute-start(f32[232,128]{1,0:T(8,128)S(1)} %pad_maximum_fusion.6.refs_2_.refs_29_), channel_id=1, source_target_pairs={{0,16},{8,24},{16,0},{24,8},{1,17},{9,25},{17,1},{25,9},{2,18},{10... | collective-permute-start | bytes 356360 | tf_op jit(solution)/shard_map/ppermute | solution.py:538
  126.8 7.4 %collective-permute-start.28 = (f32[224,128]{1,0:T(8,128)S(1)}, f32[224,128]{1,0:T(8,128)S(1)}, u32[]{:S(2)}, u32[]{:S(2)}) collective-permute-start(f32[224,128]{1,0:T(8,128)S(1)} %bitcast_add_fusion.refs_21_), channel_id=1, source_target_pairs={{0,4},{1,5},{2,6},{3,7},{4,0},{5,1},{6,2},{7,3},{8,12},{9,13},{10,... | collective-permute-start | bytes 344072 | tf_op jit(solution)/shard_map/ppermute | solution.py:538
  126.9 11.5 %collective-permute-start.30 = (f32[224,128]{1,0:T(8,128)S(1)}, f32[224,128]{1,0:T(8,128)S(1)}, u32[]{:S(2)}, u32[]{:S(2)}) collective-permute-start(f32[224,128]{1,0:T(8,128)S(1)} %bitcast_add_fusion.refs_21_), channel_id=1, source_target_pairs={{0,6},{1,7},{2,4},{3,5},{4,2},{5,3},{6,0},{7,1},{8,14},{9,15},{10,... | collective-permute-start | bytes 344072 | tf_op jit(solution)/shard_map/ppermute | solution.py:538
  128.3 12.8 %collective-permute-start.24 = (f32[232,128]{1,0:T(8,128)S(1)}, f32[232,128]{1,0:T(8,128)S(1)}, u32[]{:S(2)}, u32[]{:S(2)}) collective-permute-start(f32[232,128]{1,0:T(8,128)S(1)} %pad_maximum_fusion.6.refs_2_.refs_29_), channel_id=1, source_target_pairs={{0,24},{8,16},{16,8},{24,0},{1,25},{9,17},{17,9},{25,1},{2,26},{10... | collective-permute-start | bytes 356360 | tf_op jit(solution)/shard_map/ppermute | solution.py:538
  134.3 7.6 %collective-permute-start.25 = (f32[224,128]{1,0:T(8,128)S(1)}, f32[224,128]{1,0:T(8,128)S(1)}, u32[]{:S(2)}, u32[]{:S(2)}) collective-permute-start(f32[224,128]{1,0:T(8,128)S(1)} %bitcast_add_fusion.refs_21_), channel_id=1, source_target_pairs={{0,1},{1,0},{2,3},{3,2},{4,5},{5,4},{6,7},{7,6},{8,9},{9,8},{10,11... | collective-permute-start | bytes 344072 | tf_op jit(solution)/shard_map/ppermute | solution.py:538
  190.8 8.2 %collective-permute-start.32 = (f32[896,128]{1,0:T(8,128)}, f32[896,128]{1,0:T(8,128)S(1)}, u32[]{:S(2)}, u32[]{:S(2)}) collective-permute-start(f32[896,128]{1,0:T(8,128)} %get-tuple-element.38), channel_id=1, source_target_pairs={{0,1},{1,0},{2,3},{3,2},{4,5},{5,4},{6,7},{7,6},{8,9},{9,8},{10,11... | collective-permute-start | bytes 1376264 | tf_op jit(solution)/shard_map/ppermute | solution.py:538
  191.3 7.0 %collective-permute-start.37 = (f32[224,128]{1,0:T(8,128)S(1)}, f32[224,128]{1,0:T(8,128)S(1)}, u32[]{:S(2)}, u32[]{:S(2)}) collective-permute-start(f32[224,128]{1,0:T(8,128)S(1)} %get-tuple-element.41), channel_id=1, source_target_pairs={{0,8},{8,0},{16,24},{24,16},{1,9},{9,1},{17,25},{25,17},{2,10},{10... | collective-permute-start | bytes 344072 | tf_op jit(solution)/shard_map/ppermute | solution.py:538
  191.7 7.3 %collective-permute-start.38 = (f32[224,128]{1,0:T(8,128)S(1)}, f32[224,128]{1,0:T(8,128)S(1)}, u32[]{:S(2)}, u32[]{:S(2)}) collective-permute-start(f32[224,128]{1,0:T(8,128)S(1)} %get-tuple-element.42), channel_id=1, source_target_pairs={{0,16},{8,24},{16,0},{24,8},{1,17},{9,25},{17,1},{25,9},{2,18},{10... | collective-permute-start | bytes 344072 | tf_op jit(solution)/shard_map/ppermute | solution.py:538
  200.2 7.7 %collective-permute-start.34 = (f32[232,128]{1,0:T(8,128)S(1)}, f32[232,128]{1,0:T(8,128)S(1)}, u32[]{:S(2)}, u32[]{:S(2)}) collective-permute-start(f32[232,128]{1,0:T(8,128)S(1)} %get-tuple-element.69), channel_id=1, source_target_pairs={{0,2},{1,3},{2,0},{3,1},{4,6},{5,7},{6,4},{7,5},{8,10},{9,11},{10,... | collective-permute-start | bytes 356360 | tf_op jit(solution)/shard_map/ppermute | solution.py:538
  200.9 12.6 %collective-permute-start.35 = (f32[232,128]{1,0:T(8,128)S(1)}, f32[232,128]{1,0:T(8,128)S(1)}, u32[]{:S(2)}, u32[]{:S(2)}) collective-permute-start(f32[232,128]{1,0:T(8,128)S(1)} %get-tuple-element.70), channel_id=1, source_target_pairs={{0,4},{1,5},{2,6},{3,7},{4,0},{5,1},{6,2},{7,3},{8,12},{9,13},{10,... | collective-permute-start | bytes 356360 | tf_op jit(solution)/shard_map/ppermute | solution.py:538
  202.7 13.1 %collective-permute-start.36 = (f32[232,128]{1,0:T(8,128)S(1)}, f32[232,128]{1,0:T(8,128)S(1)}, u32[]{:S(2)}, u32[]{:S(2)}) collective-permute-start(f32[232,128]{1,0:T(8,128)S(1)} %get-tuple-element.71), channel_id=1, source_target_pairs={{0,6},{1,7},{2,4},{3,5},{4,2},{5,3},{6,0},{7,1},{8,14},{9,15},{10,... | collective-permute-start | bytes 356360 | tf_op jit(solution)/shard_map/ppermute | solution.py:538
  203.7 15.9 %collective-permute-start.40 = (f32[14,8,128]{2,1,0:T(8,128)S(1)}, f32[14,8,128]{2,1,0:T(8,128)S(1)}, u32[]{:S(2)}, u32[]{:S(2)}) collective-permute-start(f32[14,8,128]{2,1,0:T(8,128)S(1)} %get-tuple-element.57), channel_id=1, source_target_pairs={{0,0},{1,1},{2,8},{3,9},{4,16},{5,17},{6,24},{7,25},{8,2},{9,3},{1... | collective-permute-start | bytes 172040 | tf_op jit(solution)/shard_map/ppermute | solution.py:583
  207.5 12.1 %collective-permute-start.41 = (f32[14,8,128]{2,1,0:T(8,128)S(1)}, f32[14,8,128]{2,1,0:T(8,128)S(1)}, u32[]{:S(2)}, u32[]{:S(2)}) collective-permute-start(f32[14,8,128]{2,1,0:T(8,128)S(1)} %get-tuple-element.58), channel_id=1, source_target_pairs={{0,1},{1,0},{2,9},{3,8},{4,17},{5,16},{6,25},{7,24},{8,3},{9,2},{1... | collective-permute-start | bytes 172040 | tf_op jit(solution)/shard_map/ppermute | solution.py:583
  (35 other events, 835.2 us)
